TPU v7x, 32 devices: a whole 2x2x4 slice. The times are simulated.
32 devices in a mesh: row: 8 (over z, y), col: 4 (over x, core).
Axes of the slice: x: 2, y: 2, z: 4, core: 2. Of those that a mesh axis runs over, the one named last changes fastest.
Arguments:
- ancestor_inverse: float32 [12288, 12288], P('row', 'col'), may hold values from -5 to 320, as said below
- panel_one: float32 [12288, 256], P(('row', 'col')), may hold values from -0.015625 to 0.015625
- struct_one: int32 [10752], replicated, may hold values from 0 to 12287, as said below
- lower_one: float32 [256, 256], replicated, may hold values from -1 to 2, as said below
- panel_two: float32 [12288, 256], P(('row', 'col')), may hold values from -0.015625 to 0.015625
- struct_two: int32 [9216], replicated, may hold values from 0 to 12287, as said below
- panel_above: float32 [256, 256], replicated, may hold values from -0.375 to 0.375
- lower_two: float32 [256, 256], replicated, may hold values from -1 to 2, as said below
- tile_owner: int32 [192, 1], P(('col', 'row')), may hold values from 0 to 3; in each aligned block of 6 rows (0 to 5, 6 to 11, ...) at most 2 rows name the same one
Outputs:
- inverse_one: float32 [12288, 256], P(('col', 'row'))
- diag_one: float32 [256, 256], replicated
- cross_two: float32 [256, 256], replicated
- diag_two: float32 [256, 256], replicated
- delivered: float32 [256, 64, 256], P(('row', 'col'))
Inputs may be any that keep to these rules, and one draw needn't show every extreme that they name: ancestor_inverse is exactly symmetric and positive definite. `struct_one`: 10752 distinct row numbers of the ancestor block. `struct_two`: 9216 distinct entries of struct_one. `lower_one`: lower triangular with a positive diagonal. `lower_two`: lower triangular with a positive diagonal. `tile_owner`: within each aligned block of 6 entries (the tiles of one device) no value appears more than 2 times; in some block a value appears exactly 2 times.
All inputs are finite; a program needn't handle non-finite values.
Results may differ from a plain program's by a relative error of at most 0.00007.
Values sent between devices are 32-bit elements; how exact they have to be, the bound alone decides.
A program may use at most 64 MiB of HBM per device.

v0:
```python
import jax
import jax.numpy as jnp
from jax import lax
from jax.sharding import PartitionSpec as P

ANC = 12288
CAP = 2


def matmul(left, right):
    return jnp.dot(left, right, precision=lax.Precision.HIGHEST, preferred_element_type=jnp.float32)


def contract_rows(left, right):
    return lax.dot_general(
        left,
        right,
        (((0,), (0,)), ((), ())),
        precision=lax.Precision.HIGHEST,
        preferred_element_type=jnp.float32,
    )


def product_term(ancestor_inverse, block_panel, placed_rows):
    return jnp.concatenate([contract_rows(ancestor_inverse, block_panel), placed_rows], axis=1)


def deliver(values, tile_owner, col_count):
    tile_count = tile_owner.shape[0]
    tile_rows = values.shape[0] // tile_count
    all_tiles = values.reshape(tile_count, tile_rows, values.shape[1])
    owner_col = tile_owner[:, 0]
    col_ids = jnp.arange(col_count, dtype=jnp.int32)
    onehot = (owner_col[:, None] == col_ids[None, :]).astype(jnp.int32)
    tile_rank = jnp.sum((jnp.cumsum(onehot, axis=0) - onehot) * onehot, axis=1)
    slot_index = jnp.arange(CAP, dtype=jnp.int32)
    select = (
        (owner_col[None, None, :] == col_ids[:, None, None])
        & (tile_rank[None, None, :] == slot_index[None, :, None])
    ).astype(jnp.float32)
    outgoing = jnp.einsum("cks,srb->ckrb", select, all_tiles, precision=lax.Precision.HIGHEST)
    incoming = lax.all_to_all(outgoing, "col", split_axis=0, concat_axis=0, tiled=True)
    return incoming.reshape(col_count * CAP, tile_rows, values.shape[1])


def local(
    ancestor_inverse,
    panel_one,
    struct_one,
    lower_one,
    panel_two,
    struct_two,
    panel_above,
    lower_two,
    tile_owner,
):
    row_count = lax.axis_size("row")
    col_count = lax.axis_size("col")
    row_index = lax.axis_index("row")
    col_index = lax.axis_index("col")
    block_ratio = row_count // col_count
    local_rows = panel_one.shape[0]
    inner_rows = ancestor_inverse.shape[0]
    column_rows = ancestor_inverse.shape[1]
    width = panel_one.shape[1]
    mask_one = jnp.zeros((ANC,), jnp.float32).at[struct_one].set(1.0)
    mask_two = jnp.zeros((ANC,), jnp.float32).at[struct_two].set(1.0)
    panel_start = (row_index * col_count + col_index) * local_rows
    result_start = (col_index * row_count + row_index) * local_rows
    local_one = panel_one * lax.dynamic_slice_in_dim(mask_one, panel_start, local_rows)[:, None]
    local_two = panel_two * lax.dynamic_slice_in_dim(mask_two, panel_start, local_rows)[:, None]
    result_mask_one = lax.dynamic_slice_in_dim(mask_one, result_start, local_rows)[:, None]
    result_mask_two = lax.dynamic_slice_in_dim(mask_two, result_start, local_rows)[:, None]
    owns_block = (row_index // block_ratio == col_index).astype(jnp.float32)
    block_offset = row_index % block_ratio * inner_rows

    def place(gathered):
        empty_rows = jnp.zeros((column_rows, gathered.shape[1]), jnp.float32)
        return lax.dynamic_update_slice_in_dim(empty_rows, gathered * owns_block, block_offset, 0)

    gathered_one = lax.all_gather(local_one, "col", axis=0, tiled=True)
    summed_one = lax.psum_scatter(
        product_term(ancestor_inverse, gathered_one, place(gathered_one)),
        "row",
        scatter_dimension=0,
        tiled=True,
    )
    gathered_two = lax.all_gather(local_two, "col", axis=0, tiled=True)
    summed_two = lax.psum_scatter(
        product_term(ancestor_inverse, gathered_two, place(gathered_two)),
        "row",
        scatter_dimension=0,
        tiled=True,
    )
    product_one = summed_one[:, :width]
    resident_one = summed_one[:, width:]
    product_two = summed_two[:, :width]
    resident_two = summed_two[:, width:]
    inverse_one = -product_one * result_mask_one
    partial_gram = contract_rows(resident_one, inverse_one)
    partial_cross = contract_rows(inverse_one, resident_two)
    gram_one, cross_sum = lax.psum((partial_gram, partial_cross), ("row", "col"))
    diag_one = matmul(lower_one.T, lower_one) - gram_one
    cross_two = -(cross_sum + matmul(diag_one, panel_above))
    inverse_two = -(product_two + matmul(inverse_one, panel_above)) * result_mask_two
    partial_second = contract_rows(resident_two, inverse_two)
    gram_two = lax.psum(partial_second, ("row", "col"))
    diag_two = matmul(lower_two.T, lower_two) - gram_two - matmul(panel_above.T, cross_two)
    delivered = deliver(inverse_two, tile_owner, col_count)
    return (inverse_one, diag_one, cross_two, diag_two, delivered)


def solution(mesh):
    return jax.shard_map(
        local,
        mesh=mesh,
        in_specs=(
            P("row", "col"),
            P(("row", "col"), None),
            P(),
            P(),
            P(("row", "col"), None),
            P(),
            P(),
            P(),
            P(("col", "row"), None),
        ),
        out_specs=(P(("col", "row"), None), P(), P(), P(), P(("row", "col"), None, None)),
        check_vma=False,
    )
```

profile of v0, /device:TPU:0, one launch (start us, length us, event | category | flops | bytes accessed | tf_op | source)
XLA Modules:
  0.0 510.6 jit_solution(6775725624319687121)
XLA Ops:
  7.2 0.0 copy-start
  7.2 0.0 all-gather.3.cloned.1.call-start
  7.2 0.8 compare_select_fusion
  8.1 1.2 copy.36
  9.2 39.8 %scatter_custom_fusion = f32[12288]{0:T(1024)S(1)} fusion(s32[10752]{0:T(1024)S(1)} %compare_select_fusion, f32[10752]{0:T(1024)S(1)} %broadcast.48, f32[]{:T(128)} %constant.23.clone.1), kind=kCustom, calls=%fused_computation.34 | custom fusion | bytes 49156 | tf_op jit(solution)/shard_map/scatter | solution.py:66
  49.1 0.1 fusion.24
  49.2 0.8 broadcast_multiply_fusion.1
  49.9 0.0 all-gather.3.cloned.1.call-update
  50.0 0.0 all-gather.5.cloned.1.call-start
  50.0 1.2 copy.37
  51.2 0.8 compare_select_fusion.1
  52.0 34.2 %scatter_custom_fusion.1 = f32[12288]{0:T(1024)S(1)} fusion(s32[9216]{0:T(1024)S(1)} %compare_select_fusion.1, f32[9216]{0:T(1024)S(1)} %broadcast.49, f32[]{:T(128)} %constant.23.clone.1), kind=kCustom, calls=%fused_computation.32 | custom fusion | bytes 49156 | tf_op jit(solution)/shard_map/scatter | solution.py:67
  86.2 0.1 fusion.23
  86.3 0.8 broadcast_multiply_fusion
  87.0 0.0 all-gather.5.cloned.1.call-update
  87.1 0.0 reduce-scatter.3.cloned.1.call-start
  87.1 0.0 all-gather.3.cloned.1.call-done
  87.2 0.0 copy-start.1
  87.2 0.3 broadcast.46.clone
  87.5 1.0 copy-done.1
  88.6 0.1 multiply_dynamic-update-slice_fusion.1
  88.7 19.2 %convolution_bitcast_fusion.1 = f32[3072,256]{0,1:T(8,128)S(1)} fusion(f32[1536,256]{0,1:T(8,128)S(1)} %copy-done.1, f32[1536,3072]{1,0:T(8,128)} %param.9), kind=kOutput, calls=%fused_computation.5 | convolution fusion | flops 14495514624 | bytes 23592960 | tf_op jit(solution)/shard_map/dot_general | solution.py:15
  107.9 3.1 pad_maximum_fusion
  111.0 0.0 reduce-scatter.3.cloned.1.call-update
  111.0 0.2 reduce-scatter.5.cloned.1.call-start
  111.3 0.0 all-gather.5.cloned.1.call-done
  111.3 0.0 copy-start.2
  111.3 0.3 broadcast.46.clone.1
  111.6 1.0 copy-done.2
  112.7 0.1 multiply_dynamic-update-slice_fusion
  112.8 19.2 %convolution_bitcast_fusion = f32[3072,256]{0,1:T(8,128)S(1)} fusion(f32[1536,256]{0,1:T(8,128)S(1)} %copy-done.2, f32[1536,3072]{1,0:T(8,128)} %param.9), kind=kOutput, calls=%fused_computation.4 | convolution fusion | flops 14495514624 | bytes 23592960 | tf_op jit(solution)/shard_map/dot_general | solution.py:15
  132.0 3.0 pad_maximum_fusion.1
  135.1 0.0 reduce-scatter.5.cloned.1.call-update
  135.1 0.6 copy-done.9
  135.8 0.2 reduce_window_sum.11
  136.0 96.0 %reduce-scatter.3.cloned.1.call-done = f32[384,512]{0,1:T(8,128)} async-done(((f32[3072,512]{0,1:T(8,128)}), f32[384,512]{0,1:T(8,128)}) %reduce-scatter.3.cloned.1.call-update) | async-done | bytes 786448 | tf_op jit(solution)/shard_map/reduce_scatter | solution.py:82
  232.0 1.0 fusion.9
  233.0 119.7 %reduce-scatter.5.cloned.1.call-done = f32[384,512]{0,1:T(8,128)} async-done(((f32[3072,512]{0,1:T(8,128)}), f32[384,512]{0,1:T(8,128)}) %reduce-scatter.5.cloned.1.call-update) | async-done | bytes 786448 | tf_op jit(solution)/shard_map/reduce_scatter | solution.py:89
  352.7 0.0 copy-done
  352.7 1.7 fusion.1
  354.4 0.0 copy-start.8
  354.4 0.2 copy.40
  354.6 0.7 fusion.4
  355.2 0.9 copy.42
  356.1 3.6 all-to-all-start
  359.8 0.0 all-reduce.3.cloned.1.call-start
  359.8 0.0 copy-done.3
  359.8 1.3 fusion.10
  361.1 1.3 fusion.12
  362.5 0.0 copy-done.8
  362.5 1.3 fusion.7
  363.8 0.0 all-reduce.3.cloned.1.call-update
  363.8 0.9 copy.43
  364.7 3.8 all-to-all-done
  368.5 128.8 %all-reduce.3.cloned.1.call-done = (f32[256,256]{1,0:T(8,128)}, f32[256,256]{1,0:T(8,128)}, f32[256,256]{1,0:T(8,128)}) async-done(((f32[256,256]{1,0:T(8,128)}, f32[256,256]{1,0:T(8,128)}, f32[256,256]{1,0:T(8,128)}), (f32[256,256]{1,0:T(8,128)}, f32[256,256]{1,0:T(8,128)}, f32[256,256]{1,0:T(8,128)})) %all-reduce.3.cloned.1.call-update) | async-done | bytes 786448 | tf_op jit(solution)/shard_map/psum | solution.py:102
  497.3 0.0 copy-done.4
  497.3 1.5 convolution_subtract_fusion.1
  498.8 0.0 copy-start.6
  498.8 1.4 fusion.3
  500.3 0.0 copy-start.7
  500.3 0.0 copy-done.5
  500.3 1.6 convolution_subtract_fusion
  502.0 1.3 fusion.2
  503.3 0.8 copy.59
  (12 shorter events, 0.1 us)
Async XLA Ops:
  7.2 345.5 %copy-start = (f32[256,256]{1,0:T(8,128)S(1)}, f32[256,256]{1,0:T(8,128)}, u32[]{:S(2)}) copy-start(f32[256,256]{1,0:T(8,128)} %param.15) | copy-start | bytes 786436
  7.2 80.0 %all-gather.3.cloned.1.call-start = ((), (), s32[]{:S(2)}) async-start(), calls=%async_computation.3 | async-start | bytes 1966080 | tf_op jit(solution)/shard_map/all_gather | solution.py:81
  50.0 61.3 %all-gather.5.cloned.1.call-start = ((), (), s32[]{:S(2)}) async-start(), calls=%async_computation.5 | async-start | bytes 1966080 | tf_op jit(solution)/shard_map/all_gather | solution.py:88
  87.1 144.9 %reduce-scatter.3.cloned.1.call-start = ((), (), s32[]{:S(2)}) async-start(), calls=%async_computation.4 | async-start | bytes 7077888 | tf_op jit(solution)/shard_map/reduce_scatter | solution.py:82
  87.2 1.4 copy-start.1
  111.0 241.7 %reduce-scatter.5.cloned.1.call-start = ((), (), s32[]{:S(2)}) async-start(), calls=%async_computation.6 | async-start | bytes 7077888 | tf_op jit(solution)/shard_map/reduce_scatter | solution.py:89
  111.3 1.4 copy-start.2
  135.1 0.7 copy-start.9
  352.7 7.1 %copy-start.3 = (f32[384,512]{0,1:T(8,128)S(1)}, f32[384,512]{0,1:T(8,128)}, u32[]{:S(2)}) copy-start(f32[384,512]{0,1:T(8,128)} %reduce-scatter.5.cloned.1.call-done) | copy-start | bytes 2359300
  354.4 8.1 %copy-start.8 = (f32[384,512]{0,1:T(8,128)S(1)}, f32[384,512]{0,1:T(8,128)}, u32[]{:S(2)}) copy-start(f32[384,512]{0,1:T(8,128)} %reduce-scatter.3.cloned.1.call-done) | copy-start | bytes 2359300
  356.1 141.1 %copy-start.4 = (f32[256,256]{1,0:T(8,128)S(1)}, f32[256,256]{1,0:T(8,128)}, u32[]{:S(2)}) copy-start(f32[256,256]{1,0:T(8,128)} %param.12) | copy-start | bytes 786436
  356.1 12.4 %all-to-all-start = ((f32[4,2,64,256]{3,2,1,0:T(8,128)}), f32[4,2,64,256]{3,2,1,0:T(8,128)S(1)}, u32[]{:S(2)}, u32[]{:S(2)}) async-start(f32[4,2,64,256]{3,2,1,0:T(8,128)} %copy.42), calls=%async_computation.2 | async-start | bytes 1048576 | tf_op jit(solution)/shard_map/all_to_all | solution.py:42
  359.8 137.5 %all-reduce.3.cloned.1.call-start = ((), (), s32[]{:S(2)}) async-start(), calls=%async_computation.7 | async-start | bytes 1572864 | tf_op jit(solution)/shard_map/psum | solution.py:102
  361.1 139.2 %copy-start.5 = (f32[256,256]{1,0:T(8,128)S(1)}, f32[256,256]{1,0:T(8,128)}, u32[]{:S(2)}) copy-start(f32[256,256]{1,0:T(8,128)} %param.16) | copy-start | bytes 786436
  498.8 5.2 %copy-start.6 = (f32[256,256]{1,0:T(8,128)}, f32[256,256]{1,0:T(8,128)S(1)}, u32[]{:S(2)}) copy-start(f32[256,256]{1,0:T(8,128)S(1)} %convolution_subtract_fusion.1) | copy-start | bytes 786436
  500.3 3.8 copy-start.7
Sparse Core Ops, SparseCore 0:
  50.1 22.3 all-gather.2
  87.2 22.3 all-gather.4
  113.2 118.7 reduce-scatter.2
  235.4 117.2 reduce-scatter.4
  366.3 130.8 all-reduce.2
where the time goes:
time: 511 us
  waiting for transfers between devices  348 us (68%)
  local copies, waits for them, and re-layouts  82.7 us (16%)
  matrix products  50.7 us (10%)
  between operations  14.1 us (3%)
  other arithmetic  10.7 us (2%)
    psum x1, waiting for transfers between devices, local(): lax.psum((partial_gram, partial_cross), ('row', 'col'))  129 us
    reduce_scatter x1, waiting for transfers between devices, local(): lax.psum_scatter(product_term(ancestor_inverse, gathered_two, place(gathe...  120 us
    reduce_scatter x1, waiting for transfers between devices, local(): lax.psum_scatter(product_term(ancestor_inverse, gathered_one, place(gathe...  96 us
    dot_general x5, matrix products, contract_rows(): lax.dot_general(left, right, (((0,), (0,)), ((), ())), precision=lax.Prec...  42.4 us
    scatter x1, local copies, waits for them, and re-layouts, local(): mask_one = jnp.zeros((ANC,), jnp.float32).at[struct_one].set(1.0)  39.8 us
    scatter x1, local copies, waits for them, and re-layouts, local(): mask_two = jnp.zeros((ANC,), jnp.float32).at[struct_two].set(1.0)  34.2 us
  transfers between devices with their start and end apart: 6, of which 4 were waited for; matrix products, arithmetic and copies ran while one was open for 17% of the time, Pallas kernels for 0%

commit v1 on v0

--- a/solution.py
+++ b/solution.py
@@ -1,3 +1,4 @@
+import functools
 import jax
 import jax.numpy as jnp
 from jax import lax
@@ -5,6 +6,15 @@
 
 ANC = 12288
 CAP = 2
+
+
+def chains_tell(u, shard_axis, row_axis):
+    for c in (shard_axis, row_axis):
+        u = lax.psum(u, axis_name=c)
+    return u
+
+
+treat_series_all = functools.partial(chains_tell, shard_axis="col", row_axis="row")
 
 
 def matmul(left, right):
@@ -99,7 +109,7 @@
     inverse_one = -product_one * result_mask_one
     partial_gram = contract_rows(resident_one, inverse_one)
     partial_cross = contract_rows(inverse_one, resident_two)
-    gram_one, cross_sum = lax.psum((partial_gram, partial_cross), ("row", "col"))
+    gram_one, cross_sum = treat_series_all((partial_gram, partial_cross))
     diag_one = matmul(lower_one.T, lower_one) - gram_one
     cross_two = -(cross_sum + matmul(diag_one, panel_above))
     inverse_two = -(product_two + matmul(inverse_one, panel_above)) * result_mask_two

time: 511 us -> 609 us (1.19)
  waiting for transfers between devices: 348 us -> 444 us
    psum x1 -> x3, waiting for transfers between devices: 129 us -> 230 us  [the longest x1 127 us: local(): gram_two = lax.psum(partial_second, ('row', 'col'))]
  transfers between devices with their start and end apart: 6 -> 8, of which waited for: 4 -> 5; matrix products, arithmetic and copies ran while one was open for 17% -> 15% of each run, Pallas kernels for 0% -> 0%
where the time goes in v1:
time: 609 us; the launch traced here: 608 us
  waiting for transfers between devices  444 us (73%)
  local copies, waits for them, and re-layouts  82.7 us (14%)
  matrix products  52.6 us (9%)
  between operations  14.4 us (2%)
  other arithmetic  10.7 us (2%)
    psum x1, waiting for transfers between devices, local(): gram_two = lax.psum(partial_second, ('row', 'col'))  127 us
    reduce_scatter x1, waiting for transfers between devices, local(): lax.psum_scatter(product_term(ancestor_inverse, gathered_two, place(gathe...  117 us
    psum x2, waiting for transfers between devices, chains_tell(): u = lax.psum(u, axis_name=c)  104 us
    reduce_scatter x1, waiting for transfers between devices, local(): lax.psum_scatter(product_term(ancestor_inverse, gathered_one, place(gathe...  96 us
    dot_general x5, matrix products, contract_rows(): lax.dot_general(left, right, (((0,), (0,)), ((), ())), precision=lax.Prec...  44.5 us
    scatter x1, local copies, waits for them, and re-layouts, local(): mask_one = jnp.zeros((ANC,), jnp.float32).at[struct_one].set(1.0)  39.8 us
    scatter x1, local copies, waits for them, and re-layouts, local(): mask_two = jnp.zeros((ANC,), jnp.float32).at[struct_two].set(1.0)  34.2 us
  transfers between devices with their start and end apart: 8, of which 5 were waited for; matrix products, arithmetic and copies ran while one was open for 15% of the time, Pallas kernels for 0%

profile of v1, /device:TPU:0, one launch (start us, length us, event | category | flops | bytes accessed | tf_op | source)
XLA Modules:
  0.0 608.2 jit_solution(10648747044272336960)
XLA Ops:
  7.2 0.0 copy-start
  7.2 0.0 all-gather.3.cloned.1.call-start
  7.2 0.8 compare_select_fusion
  8.1 1.2 copy.36
  9.2 39.8 %scatter_custom_fusion = f32[12288]{0:T(1024)S(1)} fusion(s32[10752]{0:T(1024)S(1)} %compare_select_fusion, f32[10752]{0:T(1024)S(1)} %broadcast.48, f32[]{:T(128)} %constant.23.clone.1), kind=kCustom, calls=%fused_computation.34 | custom fusion | bytes 49156 | tf_op jit(solution)/shard_map/scatter | solution.py:76
  49.1 0.1 fusion.24
  49.2 0.8 broadcast_multiply_fusion.1
  49.9 0.0 all-gather.3.cloned.1.call-update
  50.0 0.0 all-gather.5.cloned.1.call-start
  50.0 1.2 copy.37
  51.2 0.8 compare_select_fusion.1
  52.0 34.2 %scatter_custom_fusion.1 = f32[12288]{0:T(1024)S(1)} fusion(s32[9216]{0:T(1024)S(1)} %compare_select_fusion.1, f32[9216]{0:T(1024)S(1)} %broadcast.49, f32[]{:T(128)} %constant.23.clone.1), kind=kCustom, calls=%fused_computation.32 | custom fusion | bytes 49156 | tf_op jit(solution)/shard_map/scatter | solution.py:77
  86.2 0.1 fusion.23
  86.3 0.8 broadcast_multiply_fusion
  87.0 0.0 all-gather.5.cloned.1.call-update
  87.1 0.0 reduce-scatter.3.cloned.1.call-start
  87.1 0.0 all-gather.3.cloned.1.call-done
  87.2 0.3 broadcast.46.clone
  87.5 1.0 copy-done.1
  88.6 0.1 multiply_dynamic-update-slice_fusion.1
  88.7 19.2 %convolution_bitcast_fusion.1 = f32[3072,256]{0,1:T(8,128)S(1)} fusion(f32[1536,256]{0,1:T(8,128)S(1)} %copy-done.1, f32[1536,3072]{1,0:T(8,128)} %param.9), kind=kOutput, calls=%fused_computation.5 | convolution fusion | flops 14495514624 | bytes 23592960 | tf_op jit(solution)/shard_map/dot_general | solution.py:25
  107.9 3.1 pad_maximum_fusion
  111.0 0.0 reduce-scatter.3.cloned.1.call-update
  111.0 0.2 reduce-scatter.5.cloned.1.call-start
  111.2 0.0 all-gather.5.cloned.1.call-done
  111.3 0.3 broadcast.46.clone.1
  111.6 1.0 copy-done.2
  112.7 0.1 multiply_dynamic-update-slice_fusion
  112.8 19.2 %convolution_bitcast_fusion = f32[3072,256]{0,1:T(8,128)S(1)} fusion(f32[1536,256]{0,1:T(8,128)S(1)} %copy-done.2, f32[1536,3072]{1,0:T(8,128)} %param.9), kind=kOutput, calls=%fused_computation.4 | convolution fusion | flops 14495514624 | bytes 23592960 | tf_op jit(solution)/shard_map/dot_general | solution.py:25
  132.0 3.0 pad_maximum_fusion.1
  135.1 0.0 reduce-scatter.5.cloned.1.call-update
  135.1 0.0 all-reduce.10.cloned.1.call-start
  135.2 0.6 copy-done.8
  135.8 0.2 reduce_window_sum.11
  136.0 96.0 %reduce-scatter.3.cloned.1.call-done = f32[384,512]{0,1:T(8,128)} async-done(((f32[3072,512]{0,1:T(8,128)}), f32[384,512]{0,1:T(8,128)}) %reduce-scatter.3.cloned.1.call-update) | async-done | bytes 786448 | tf_op jit(solution)/shard_map/reduce_scatter | solution.py:92
  231.9 1.0 fusion.9
  233.0 2.3 fusion.7
  235.3 117.4 %reduce-scatter.5.cloned.1.call-done = f32[384,512]{0,1:T(8,128)} async-done(((f32[3072,512]{0,1:T(8,128)}), f32[384,512]{0,1:T(8,128)}) %reduce-scatter.5.cloned.1.call-update) | async-done | bytes 786448 | tf_op jit(solution)/shard_map/reduce_scatter | solution.py:99
  352.7 2.4 fusion.12
  355.1 0.0 all-reduce.10.cloned.1.call-update
  355.1 0.0 all-reduce.6.cloned.1.call-start
  355.2 1.6 fusion.1
  356.8 0.0 copy-start.4
  356.8 1.3 fusion.10
  358.1 0.0 all-reduce.6.cloned.1.call-update
  358.2 0.0 all-reduce.8.cloned.1.call-start
  358.2 0.0 copy-start.5
  358.2 0.2 copy.40
  358.4 29.9 %all-reduce.10.cloned.1.call-done = (f32[256,256]{1,0:T(8,128)}, f32[256,256]{1,0:T(8,128)}) async-done(((f32[256,256]{1,0:T(8,128)}, f32[256,256]{1,0:T(8,128)}), (f32[256,256]{1,0:T(8,128)}, f32[256,256]{1,0:T(8,128)})) %all-reduce.10.cloned.1.call-update) | async-done | bytes 524304 | tf_op jit(solution)/shard_map/psum | solution.py:13
  388.3 0.0 all-reduce.8.cloned.1.call-update
  388.3 0.7 fusion.4
  389.0 0.9 copy.42
  389.9 3.5 all-to-all-start
  393.4 0.9 copy.43
  394.3 126.6 %all-reduce.6.cloned.1.call-done = f32[256,256]{1,0:T(8,128)} async-done(((f32[256,256]{1,0:T(8,128)}), f32[256,256]{1,0:T(8,128)}) %all-reduce.6.cloned.1.call-update) | async-done | bytes 262160 | tf_op jit(solution)/shard_map/psum | solution.py:117
  520.9 1.5 convolution_subtract_fusion
  522.5 0.0 all-to-all-done
  522.5 73.7 %all-reduce.8.cloned.1.call-done = (f32[256,256]{1,0:T(8,128)}, f32[256,256]{1,0:T(8,128)}) async-done(((f32[256,256]{1,0:T(8,128)}, f32[256,256]{1,0:T(8,128)}), (f32[256,256]{1,0:T(8,128)}, f32[256,256]{1,0:T(8,128)})) %all-reduce.8.cloned.1.call-update) | async-done | bytes 524304 | tf_op jit(solution)/shard_map/psum | solution.py:13
  596.2 1.5 convolution_subtract_fusion.1
  597.8 0.0 copy-start.6
  597.8 1.4 fusion.3
  599.2 0.0 copy-start.7
  599.2 1.3 fusion.2
  600.5 0.8 copy.61
  (16 shorter events, 0.1 us)
Async XLA Ops:
  7.2 348.0 %copy-start = (f32[256,256]{1,0:T(8,128)S(1)}, f32[256,256]{1,0:T(8,128)}, u32[]{:S(2)}) copy-start(f32[256,256]{1,0:T(8,128)} %param.15) | copy-start | bytes 786436
  7.2 80.0 %all-gather.3.cloned.1.call-start = ((), (), s32[]{:S(2)}) async-start(), calls=%async_computation.3 | async-start | bytes 1966080 | tf_op jit(solution)/shard_map/all_gather | solution.py:91
  50.0 61.3 %all-gather.5.cloned.1.call-start = ((), (), s32[]{:S(2)}) async-start(), calls=%async_computation.5 | async-start | bytes 1966080 | tf_op jit(solution)/shard_map/all_gather | solution.py:98
  87.1 144.9 %reduce-scatter.3.cloned.1.call-start = ((), (), s32[]{:S(2)}) async-start(), calls=%async_computation.4 | async-start | bytes 7077888 | tf_op jit(solution)/shard_map/reduce_scatter | solution.py:92
  87.2 1.4 copy-start.1
  111.0 241.7 %reduce-scatter.5.cloned.1.call-start = ((), (), s32[]{:S(2)}) async-start(), calls=%async_computation.6 | async-start | bytes 7077888 | tf_op jit(solution)/shard_map/reduce_scatter | solution.py:99
  111.3 1.4 copy-start.2
  135.1 0.7 copy-start.8
  135.1 253.2 %all-reduce.10.cloned.1.call-start = ((), (), s32[]{:S(2)}) async-start(), calls=%async_computation.9 | async-start | bytes 1048576 | tf_op jit(solution)/shard_map/psum | solution.py:13
  352.7 4.1 copy-start.3
  355.1 165.8 %all-reduce.6.cloned.1.call-start = ((), (), s32[]{:S(2)}) async-start(), calls=%async_computation.7 | async-start | bytes 524288 | tf_op jit(solution)/shard_map/psum | solution.py:117
  356.8 164.1 %copy-start.4 = (f32[256,256]{1,0:T(8,128)S(1)}, f32[256,256]{1,0:T(8,128)}, u32[]{:S(2)}) copy-start(f32[256,256]{1,0:T(8,128)} %param.16) | copy-start | bytes 786436
  358.2 238.1 %all-reduce.8.cloned.1.call-start = ((), (), s32[]{:S(2)}) async-start(), calls=%async_computation.8 | async-start | bytes 1048576 | tf_op jit(solution)/shard_map/psum | solution.py:13
  358.2 238.0 %copy-start.5 = (f32[256,256]{1,0:T(8,128)S(1)}, f32[256,256]{1,0:T(8,128)}, u32[]{:S(2)}) copy-start(f32[256,256]{1,0:T(8,128)} %param.12) | copy-start | bytes 786436
  389.9 132.6 %all-to-all-start = ((f32[4,2,64,256]{3,2,1,0:T(8,128)}), f32[4,2,64,256]{3,2,1,0:T(8,128)S(1)}, u32[]{:S(2)}, u32[]{:S(2)}) async-start(f32[4,2,64,256]{3,2,1,0:T(8,128)} %copy.42), calls=%async_computation.2 | async-start | bytes 1048576 | tf_op jit(solution)/shard_map/all_to_all | solution.py:52
  597.8 3.6 copy-start.6
  599.2 2.1 copy-start.7
Sparse Core Ops, SparseCore 0:
  50.1 22.3 all-gather.2
  87.2 22.3 all-gather.4
  113.2 118.7 reduce-scatter.2
  235.4 117.2 reduce-scatter.4
  355.5 32.7 all-reduce.9
  394.2 126.6 all-reduce.5
  524.4 71.7 all-reduce.7
